TPU v7x, 512 devices: a whole 4x4x16 slice. The times are simulated.
512 devices in a mesh: gr: 16 (over y, z_hi), gc: 32 (over z_lo, x, core).
Axes of the slice: x: 4, y: 4, z: 16 (z_hi: 4, z_lo: 4; z = z_hi * 4 + z_lo), core: 2. Of those that a mesh axis runs over, the one named last changes fastest.
Arguments:
- phase: bfloat16 [2, 12288, 2048], P(None, 'gr', 'gc'), may hold values from -0.59765625 to 0.59765625
- data: bfloat16 [2, 2048, 128], P(None, 'gc'), may hold values from -6 to 6
- column_ids: int32 [2048], replicated, may hold values from 0 to 8191
- noise_weight: float32 [8192], replicated, may hold values from 0.3 to 3
Outputs:
- fisher: float32 [12288, 12288], P('gr', 'gc')
- dirty_maps: float32 [12288, 128], P(('gr', 'gc'))
All inputs are finite; a program needn't handle non-finite values.
Results may differ from a plain program's by a relative error of at most 0.0029.
Values may be sent and summed in bfloat16 or wider, within the bound.
No kernel may reach another device: no remote copies, remote signals or barrier semaphores. Data moves between devices by JAX's collectives and lax.ppermute only.
A program may use at most 64 MiB of HBM per device.

v0:
```python
import jax
import jax.numpy as jnp
from jax import lax
from jax.sharding import PartitionSpec as P


def from_root(block, axis, source):
    block = jnp.where(lax.axis_index(axis) == source, block, jnp.zeros_like(block))
    return lax.psum(block, axis)


def shards(phase, data, column_ids, noise_weight):
    grid_rows = lax.axis_size("gr")
    grid_cols = lax.axis_size("gc")
    col_index = lax.axis_index("gc")
    local_cols = phase.shape[2]
    left_count = phase.shape[1]
    right_count = left_count * grid_rows // grid_cols
    ratio = grid_cols // grid_rows
    weight = jnp.take(noise_weight, column_ids)
    left = lax.all_gather(phase, "gc", axis=2, tiled=True)
    offset = col_index % ratio * right_count
    root = col_index // ratio
    piece = lax.dynamic_slice_in_dim(left, offset, right_count, 1)
    received = from_root(piece, "gr", root)
    weighted_right = (received.astype(jnp.float32) * weight).astype(jnp.bfloat16)
    fisher = lax.dot_general(
        left, weighted_right, (((0, 2), (0, 2)), ((), ())), preferred_element_type=jnp.float32
    )
    local_weight = lax.dynamic_slice_in_dim(weight, col_index * local_cols, local_cols, 0)
    weighted_local = (phase.astype(jnp.float32) * local_weight).astype(jnp.bfloat16)
    partial_maps = lax.dot_general(
        weighted_local, data, (((0, 2), (0, 1)), ((), ())), preferred_element_type=jnp.float32
    )
    dirty_maps = lax.psum_scatter(partial_maps, "gc", scatter_dimension=0, tiled=True)
    return (fisher, dirty_maps)


def solution(mesh):
    return jax.shard_map(
        shards,
        mesh=mesh,
        in_specs=(P(None, "gr", "gc"), P(None, "gc", None), P(), P()),
        out_specs=(P("gr", "gc"), P(("gr", "gc"), None)),
        check_vma=False,
    )
```

profile of v0, /device:TPU:8, one launch (start us, length us, event | category | flops | bytes accessed | tf_op | source)
XLA Modules:
  0.0 571.2 jit_solution(10424257190026620569)
XLA Ops:
  7.2 0.0 copy-start
  7.2 0.0 all-gather.2.cloned.1.call-start
  7.2 0.7 all-gather.2.cloned.1.call-update
  7.9 0.0 all-reduce.3.cloned.1.call-start
  8.0 77.1 %all-gather.2.cloned.1.call-done = bf16[2,768,2048]{1,2,0:T(8,128)(2,1)} async-done(((bf16[2,768,64]{1,2,0:T(8,128)(2,1)}), bf16[2,768,2048]{1,2,0:T(8,128)(2,1)}) %all-gather.2.cloned.1.call-update) | async-done | bytes 6291472 | tf_op jit(solution)/shard_map/all_gather | solution.py:21
  85.1 4.1 dynamic-slice_select_fusion
  89.2 0.0 copy-start.3
  89.2 0.0 copy-start.1
  89.2 0.0 all-reduce.3.cloned.1.call-update
  89.3 0.0 reduce-scatter.5.cloned.1.call-start
  89.3 0.6 copy-done.3
  89.9 0.1 copy-done.1
  90.0 0.0 copy-start.2
  90.0 11.8 %gather_fusion = f32[2048]{0:T(1024)S(1)} fusion(f32[8192]{0:T(1024)S(1)} %copy-done.1, s32[2048]{0:T(1024)S(1)} %fusion.4), kind=kCustom, calls=%fused_computation | custom fusion | bytes 24576 | tf_op jit(solution)/shard_map/jit(_take)/gather | solution.py:20
  101.8 0.1 dynamic_slice.7
  101.9 0.0 copy-done
  101.9 0.0 copy-done.2
  101.9 1.1 convolution_bitcast_fusion
  103.0 0.0 reduce-scatter.5.cloned.1.call-update
  103.0 308.5 %all-reduce.3.cloned.1.call-done = bf16[2,384,2048]{1,2,0:T(8,128)(2,1)} async-done(((bf16[2,384,2048]{1,2,0:T(8,128)(2,1)}), bf16[2,384,2048]{1,2,0:T(8,128)(2,1)}) %all-reduce.3.cloned.1.call-update) | async-done | bytes 3145744 | tf_op jit(solution)/shard_map/psum | solution.py:9
  411.5 6.5 %fusion.2 = f32[768,384]{0,1:T(8,128)S(1)} fusion(bf16[2,768,2048]{1,2,0:T(8,128)(2,1)} %all-gather.2.cloned.1.call-done, bf16[2,384,2048]{1,2,0:T(8,128)(2,1)} %all-reduce.3.cloned.1.call-done, f32[2048]{0:T(1024)S(1)} %and_select_fusion), kind=kOutput, calls=%fused_computation.5 | convolution fusion | flops 2420637696 | bytes 10625024 | tf_op jit(solution)/shard_map/dot_general | solution.py:27
  418.0 1.4 copy.11
  419.4 145.3 %reduce-scatter.5.cloned.1.call-done = f32[24,128]{1,0:T(8,128)} async-done(((f32[768,128]{1,0:T(8,128)}), f32[24,128]{1,0:T(8,128)}) %reduce-scatter.5.cloned.1.call-update) | async-done | bytes 12304
  (2 shorter events, 0.0 us)
Async XLA Ops:
  7.2 94.7 %copy-start = (bf16[2,64,128]{2,1,0:T(8,128)(2,1)S(1)}, bf16[2,64,128]{2,1,0:T(8,128)(2,1)}, u32[]{:S(2)}) copy-start(bf16[2,64,128]{2,1,0:T(8,128)(2,1)} %param.5) | copy-start | bytes 98308
  7.2 77.9 %all-gather.2.cloned.1.call-start = ((), (), s32[]{:S(2)}) async-start(), calls=%async_computation.1 | async-start | bytes 6488064 | tf_op jit(solution)/shard_map/all_gather | solution.py:21
  7.9 403.6 %all-reduce.3.cloned.1.call-start = ((), (), s32[]{:S(2)}) async-start(), calls=%async_computation.2 | async-start | bytes 6291456 | tf_op jit(solution)/shard_map/psum | solution.py:9
  89.2 0.7 copy-start.3
  89.2 0.8 copy-start.1
  89.3 475.4 %reduce-scatter.5.cloned.1.call-start = ((), (), s32[]{:S(2)}) async-start(), calls=%async_computation.3 | async-start | bytes 405504
  90.0 11.9 %copy-start.2 = (bf16[2,768,64]{1,2,0:T(8,128)(2,1)S(1)}, bf16[2,768,64]{1,2,0:T(8,128)(2,1)}, u32[]{:S(2)}) copy-start(bf16[2,768,64]{1,2,0:T(8,128)(2,1)} %param.4) | copy-start | bytes 589828
Sparse Core Ops, SparseCore 0:
  10.1 74.9 all-gather.1
  89.4 322.0 all-reduce.2
  414.8 149.7 reduce-scatter.4
where the time goes:
time: 571 us
  waiting for transfers between devices  532 us (93%)
  local copies, waits for them, and re-layouts  13.9 us (2%)
  between operations  13.8 us (2%)
  matrix products  7.59 us (1%)
    psum x1, waiting for transfers between devices, from_root(): return lax.psum(block, axis)  308 us
    unnamed x4, waiting for transfers between devices  146 us
    all_gather x1, waiting for transfers between devices, shards(): left = lax.all_gather(phase, 'gc', axis=2, tiled=True)  77.1 us
    gather x1, local copies, waits for them, and re-layouts, shards(): weight = jnp.take(noise_weight, column_ids)  11.8 us
  transfers between devices with their start and end apart: 3, of which 3 were waited for; matrix products, arithmetic and copies ran while one was open for 4% of the time, Pallas kernels for 0%

commit v1 on v0

v1 whole, which is shorter than its diff:
```python
import itertools

import jax
import jax.numpy as jnp
from jax import lax
from jax.sharding import Mesh, PartitionSpec as P

AXES = ("y", "zh", "zl", "x", "c")


def turned(other_core):
    pairs = []
    for source, (y, zh, zl, x, c) in enumerate(itertools.product(range(4), range(4), range(4), range(4), range(2))):
        core = 1 - c if other_core else c
        pairs.append((source, (((zl * 4 + x) * 4 + y) * 4 + zh) * 2 + core))
    return pairs


def shards(phase, data, column_ids, noise_weight):
    core = lax.axis_index("c")
    group = (lax.axis_index("zl") * 4 + lax.axis_index("x")) * 2 + core
    rows, cols = phase.shape[1], phase.shape[2]
    half = rows // 2
    local = jnp.transpose(phase, (0, 2, 1))
    mine = lax.dynamic_slice_in_dim(local, core * half, half, 2)
    other = lax.dynamic_slice_in_dim(local, (1 - core) * half, half, 2)
    mine = lax.ppermute(mine, AXES, turned(False))
    other = lax.ppermute(other, AXES, turned(True))
    first = jnp.where(core == 0, mine, other)
    second = jnp.where(core == 0, other, mine)
    pair = jnp.stack([first, second])
    left = lax.all_gather(local, ("zl", "x", "c"), axis=0)
    across = lax.all_gather(pair, "zh", axis=0)
    pieces = [lax.all_gather(across[k], "y", axis=0) for k in range(4)]
    right = jnp.stack(pieces, axis=1)
    weight = jnp.take(noise_weight, column_ids, mode="clip").reshape(4, 4, 2, 1, cols, 1)
    right = (right.astype(jnp.float32) * weight).astype(jnp.bfloat16)
    fisher = lax.dot_general(
        left.reshape(-1, rows), right.reshape(-1, half), (((0,), (0,)), ((), ())), preferred_element_type=jnp.float32
    )
    local_weight = lax.dynamic_slice_in_dim(weight.reshape(-1), group * cols, cols, 0)
    weighted = (local.astype(jnp.float32) * local_weight[:, None]).astype(jnp.bfloat16)
    partial = lax.dot_general(
        weighted, data, (((0, 1), (0, 1)), ((), ())), preferred_element_type=jnp.float32
    )
    partial = partial.reshape(32, rows // 32, -1)
    parts = lax.all_to_all(partial, ("zl", "x", "c"), 0, 0)
    dirty_maps = jnp.sum(parts, axis=0)
    return fisher, dirty_maps


def solution(mesh):
    fine = Mesh(mesh.devices.reshape(4, 4, 4, 4, 2), AXES)
    return jax.shard_map(
        shards,
        mesh=fine,
        in_specs=(P(None, ("y", "zh"), ("zl", "x", "c")), P(None, ("zl", "x", "c"), None), P(), P()),
        out_specs=(P(("y", "zh"), ("zl", "x", "c")), P(AXES, None)),
        check_vma=False,
    )
```

time: 571 us -> 188 us (0.33)
  the two profiles are of different devices: /device:TPU:8 before, /device:TPU:34 now
where the time goes in v1:
time: 188 us; the launch traced here: 187 us
  blocking collectives  117 us (62%)
  starting transfers between devices  24.8 us (13%)
  local copies, waits for them, and re-layouts  15.7 us (8%)
  between operations  14.1 us (8%)
  matrix products  7.51 us (4%)
  waiting for transfers between devices  4.74 us (3%)
  other arithmetic  3.34 us (2%)
    all_gather x4, blocking collectives, shards(): pieces = [lax.all_gather(across[k], 'y', axis=0) for k in range(4)]  69 us
    all_gather x1, blocking collectives, shards(): across = lax.all_gather(pair, 'zh', axis=0)  47.9 us
    all_to_all x1, starting transfers between devices, shards(): parts = lax.all_to_all(partial, ('zl', 'x', 'c'), 0, 0)  14.2 us
    gather x1, local copies, waits for them, and re-layouts, shards(): jnp.take(noise_weight, column_ids, mode='clip').reshape(4, 4, 2, 1, cols, 1)  11.8 us
    ppermute x1, starting transfers between devices, shards(): mine = lax.ppermute(mine, AXES, turned(False))  8.73 us
    dot_general x1, matrix products, shards(): lax.dot_general(left.reshape(-1, rows), right.reshape(-1, half), (((0,),...  6.46 us
  transfers between devices with their start and end apart: 4, of which 2 were waited for; matrix products, arithmetic and copies ran while one was open for 9% of the time, Pallas kernels for 0%

profile of v1, /device:TPU:34, one launch (start us, length us, event | category | flops | bytes accessed | tf_op | source)
XLA Modules:
  0.0 187.1 jit_solution(12613920560077180221)
XLA Ops:
  7.2 0.0 copy-start
  7.2 0.0 copy-start.1
  7.2 0.0 all-gather.8.cloned.1.call-start
  7.2 0.7 all-gather.8.cloned.1.call-update
  7.9 1.0 dynamic-slice_bitcast_fusion.1
  8.9 8.7 %collective-permute-start = (bf16[2,64,384]{2,1,0:T(8,128)(2,1)S(1)}, bf16[2,64,384]{2,1,0:T(8,128)(2,1)S(1)}, u32[]{:S(2)}, u32[]{:S(2)}) collective-permute-start(bf16[2,64,384]{2,1,0:T(8,128)(2,1)S(1)} %get-tuple-element.14), channel_id=1, source_target_pairs={{0,0},{1,1},{2,32},{3,33},{4,64},{5,65},{6,96},{7,97},{8,128},{9,1... | collective-permute-start | bytes 294920 | tf_op jit(solution)/shard_map/ppermute | solution.py:27
  17.6 1.9 %collective-permute-start.1 = (bf16[2,64,384]{2,1,0:T(8,128)(2,1)S(1)}, bf16[2,64,384]{2,1,0:T(8,128)(2,1)S(1)}, u32[]{:S(2)}, u32[]{:S(2)}) collective-permute-start(bf16[2,64,384]{2,1,0:T(8,128)(2,1)S(1)} %get-tuple-element.15), channel_id=1, source_target_pairs={{0,1},{1,0},{2,33},{3,32},{4,65},{5,64},{6,97},{7,96},{8,129},{9,1... | collective-permute-start | bytes 294920 | tf_op jit(solution)/shard_map/ppermute | solution.py:28
  19.6 0.7 broadcast_clamp_fusion
  20.3 0.0 copy-done.1
  20.3 0.0 copy-start.2
  20.3 11.8 %gather_fusion = f32[2048]{0:T(1024)S(1)} fusion(f32[8192]{0:T(1024)S(1)} %copy-done.1, s32[2048]{0:T(1024)S(1)} %broadcast_clamp_fusion), kind=kCustom, calls=%fused_computation | custom fusion | bytes 24576 | tf_op jit(solution)/shard_map/jit(_take)/gather | solution.py:36
  32.1 0.1 dynamic_slice.11
  32.1 0.0 copy-done
  32.2 0.0 copy-done.2
  32.2 1.1 fusion
  33.2 14.2 %all-to-all-start = ((f32[32,24,128]{2,1,0:T(8,128)}), f32[32,24,128]{2,1,0:T(8,128)}, u32[]{:S(2)}, u32[]{:S(2)}) async-start(f32[32,24,128]{2,1,0:T(8,128)} %bitcast.13), calls=%async_computation | async-start | bytes 786432 | tf_op jit(solution)/shard_map/all_to_all | solution.py:47
  47.4 0.1 mul.43
  47.5 3.2 %collective-permute-done = bf16[2,64,384]{2,1,0:T(8,128)(2,1)S(1)} collective-permute-done((bf16[2,64,384]{2,1,0:T(8,128)(2,1)S(1)}, bf16[2,64,384]{2,1,0:T(8,128)(2,1)S(1)}, u32[]{:S(2)}, u32[]{:S(2)}) %collective-permute-start) | collective-permute-done | bytes 98336 | tf_op jit(solution)/shard_map/ppermute | solution.py:27
  50.7 0.8 collective-permute-done.1
  51.6 47.9 %all-gather = bf16[8,2,64,384]{3,2,1,0:T(8,128)(2,1)S(1)} all-gather(bf16[2,2,64,384]{3,2,1,0:T(8,128)(2,1)S(1)} %pad_maximum_fusion), channel_id=2, replica_groups=mesh['y'=4,'zh'=4,'zl'=4,'x'=4,'c'=2] {'zh'}, dimensions={0}, use_global_device_ids=true | all-gather | bytes 983040 | tf_op jit(solution)/shard_map/all_gather | solution.py:33
  99.5 0.1 fusion.3
  99.6 26.5 %all-gather.2 = bf16[8,2,64,384]{3,2,1,0:T(8,128)(2,1)S(1)} all-gather(bf16[2,2,64,384]{3,2,1,0:T(8,128)(2,1)S(1)} %get-tuple-element.8), channel_id=4, replica_groups=mesh['y'=4,'zh'=4,'zl'=4,'x'=4,'c'=2] {'y'}, dimensions={0}, use_global_device_ids=true | all-gather | bytes 983040 | tf_op jit(solution)/shard_map/all_gather | solution.py:34
  126.1 14.9 %all-gather.3 = bf16[8,2,64,384]{3,2,1,0:T(8,128)(2,1)S(1)} all-gather(bf16[2,2,64,384]{3,2,1,0:T(8,128)(2,1)S(1)} %get-tuple-element.10), channel_id=5, replica_groups=mesh['y'=4,'zh'=4,'zl'=4,'x'=4,'c'=2] {'y'}, dimensions={0}, use_global_device_ids=true | all-gather | bytes 983040 | tf_op jit(solution)/shard_map/all_gather | solution.py:34
  140.9 14.3 %all-gather.4 = bf16[8,2,64,384]{3,2,1,0:T(8,128)(2,1)S(1)} all-gather(bf16[2,2,64,384]{3,2,1,0:T(8,128)(2,1)S(1)} %get-tuple-element.9), channel_id=6, replica_groups=mesh['y'=4,'zh'=4,'zl'=4,'x'=4,'c'=2] {'y'}, dimensions={0}, use_global_device_ids=true | all-gather | bytes 983040 | tf_op jit(solution)/shard_map/all_gather | solution.py:34
  155.3 13.3 %all-gather.5 = bf16[8,2,64,384]{3,2,1,0:T(8,128)(2,1)S(1)} all-gather(bf16[2,2,64,384]{3,2,1,0:T(8,128)(2,1)S(1)} %get-tuple-element.11), channel_id=7, replica_groups=mesh['y'=4,'zh'=4,'zl'=4,'x'=4,'c'=2] {'y'}, dimensions={0}, use_global_device_ids=true | all-gather | bytes 983040 | tf_op jit(solution)/shard_map/all_gather | solution.py:34
  168.6 0.9 multiply_convert_fusion
  169.5 0.0 all-to-all-done
  169.5 1.6 reduce_sum.9
  171.2 0.0 all-gather.8.cloned.1.call-done
  171.2 6.5 %convolution_bitcast_fusion = f32[768,384]{0,1:T(8,128)} fusion(bf16[4096,384]{1,0:T(8,128)(2,1)S(1)} %bitcast.27, bf16[4096,768]{1,0:T(8,128)(2,1)} %bitcast.28), kind=kOutput, calls=%fused_computation.2 | convolution fusion | flops 2415919104 | bytes 10616832 | tf_op jit(solution)/shard_map/dot_general | solution.py:38
  177.6 2.7 %copy.8 = f32[768,384]{1,0:T(8,128)} copy(f32[768,384]{0,1:T(8,128)} %convolution_bitcast_fusion) | data formatting | bytes 2359296
  (2 shorter events, 0.1 us)
Async XLA Ops:
  7.2 25.0 %copy-start = (bf16[2,64,128]{2,1,0:T(8,128)(2,1)S(1)}, bf16[2,64,128]{2,1,0:T(8,128)(2,1)}, u32[]{:S(2)}) copy-start(bf16[2,64,128]{2,1,0:T(8,128)(2,1)} %param.5) | copy-start | bytes 98308
  7.2 13.1 %copy-start.1 = (f32[8192]{0:T(1024)S(1)}, f32[8192]{0:T(1024)}, u32[]{:S(2)}) copy-start(f32[8192]{0:T(1024)} %param.7) | copy-start | bytes 98308
  7.2 164.0 %all-gather.8.cloned.1.call-start = ((), (), s32[]{:S(2)}) async-start(), calls=%async_computation.1 | async-start | bytes 6488064 | tf_op jit(solution)/shard_map/all_gather | solution.py:32
  8.9 41.8 %collective-permute-start = (bf16[2,64,384]{2,1,0:T(8,128)(2,1)S(1)}, bf16[2,64,384]{2,1,0:T(8,128)(2,1)S(1)}, u32[]{:S(2)}, u32[]{:S(2)}) collective-permute-start(bf16[2,64,384]{2,1,0:T(8,128)(2,1)S(1)} %get-tuple-element.14), channel_id=1, source_target_pairs={{0,0},{1,1},{2,32},{3,33},{4,64},{5,65},{6,96},{7,97},{8,128},{9,1... | collective-permute-start | bytes 294920 | tf_op jit(solution)/shard_map/ppermute | solution.py:27
  17.6 33.9 %collective-permute-start.1 = (bf16[2,64,384]{2,1,0:T(8,128)(2,1)S(1)}, bf16[2,64,384]{2,1,0:T(8,128)(2,1)S(1)}, u32[]{:S(2)}, u32[]{:S(2)}) collective-permute-start(bf16[2,64,384]{2,1,0:T(8,128)(2,1)S(1)} %get-tuple-element.15), channel_id=1, source_target_pairs={{0,1},{1,0},{2,33},{3,32},{4,65},{5,64},{6,97},{7,96},{8,129},{9,1... | collective-permute-start | bytes 294920 | tf_op jit(solution)/shard_map/ppermute | solution.py:28
  20.3 11.9 %copy-start.2 = (bf16[2,768,64]{1,2,0:T(8,128)(2,1)S(1)}, bf16[2,768,64]{1,2,0:T(8,128)(2,1)}, u32[]{:S(2)}) copy-start(bf16[2,768,64]{1,2,0:T(8,128)(2,1)} %param.4) | copy-start | bytes 589828
  33.2 136.3 %all-to-all-start = ((f32[32,24,128]{2,1,0:T(8,128)}), f32[32,24,128]{2,1,0:T(8,128)}, u32[]{:S(2)}, u32[]{:S(2)}) async-start(f32[32,24,128]{2,1,0:T(8,128)} %bitcast.13), calls=%async_computation | async-start | bytes 786432 | tf_op jit(solution)/shard_map/all_to_all | solution.py:47
Sparse Core Ops, SparseCore 0:
  10.1 116.4 all-gather.7

commit v2 on v1

v2 whole, which is shorter than its diff:
```python
import jax
import jax.numpy as jnp
from jax import lax
from jax.sharding import Mesh, PartitionSpec as P

AXES = ("y", "zh", "zl", "x", "c")


def send(block, axis, step):
    return lax.ppermute(block, axis, [(i, (i + step) % 4) for i in range(4)])


def gather(block, axis):
    return lax.all_gather(block, axis, axis=0)


def table_rows(noise_weight, column_ids):
    table = noise_weight.reshape(-1, 128)
    high, low = column_ids >> 7, column_ids & 127
    pick = (lax.broadcasted_iota(jnp.int32, (table.shape[0], high.shape[0]), 0) == high[None]).astype(jnp.float32)
    lanes = lax.dot_general(
        table, pick, (((0,), (0,)), ((), ())), precision=lax.Precision.HIGHEST, preferred_element_type=jnp.float32
    )
    keep = lax.broadcasted_iota(jnp.int32, lanes.shape, 0) == low[None]
    return jnp.sum(jnp.where(keep, lanes, 0.0), axis=0)


def step(phase, data, column_ids, noise_weight):
    core = lax.axis_index("c")
    zl, x = lax.axis_index("zl"), lax.axis_index("x")
    rows, cols = phase.shape[1], phase.shape[2]
    half = rows // 2
    local = jnp.transpose(phase, (0, 2, 1))
    own = lax.ppermute(local, ("y", "zl"), [(4 * i + j, 4 * j + i) for i in range(4) for j in range(4)])
    line = gather(jnp.concatenate([local, data], axis=2), "zl")
    xprev = send(line, "x", 1)
    xsucc = send(line, "x", -1)
    xfar = send(line, "x", 2)
    across = gather(own, "zh")
    line, across = lax.optimization_barrier((line, across))
    spread = jnp.stack([across[..., :half], across[..., half:]], axis=1)
    spread = jnp.broadcast_to(spread, (4,) + spread.shape).reshape((32,) + spread.shape[2:])
    right = lax.all_to_all(spread, ("y", "x", "c"), 0, 0)
    weight = table_rows(noise_weight, column_ids).reshape(4, 4, 2, cols)
    left = jnp.zeros((4, 4, 2) + local.shape, jnp.bfloat16)
    seen = jnp.zeros((4, 4, 2) + data.shape, jnp.bfloat16)
    for offset, piece in ((0, line), (-1, xprev), (1, xsucc), (2, xfar)):
        place = (x + offset) % 4
        twin = lax.ppermute(piece, "c", [(0, 1), (1, 0)])
        for which, block in ((core, piece), (1 - core, twin)):
            block = block[:, None, None]
            left = lax.dynamic_update_slice(left, block[..., :rows], (0, place, which, 0, 0, 0))
            seen = lax.dynamic_update_slice(seen, block[..., rows:], (0, place, which, 0, 0, 0))
    over = (((0,), (0,)), ((), ()))
    share = rows // 32
    scale = weight.reshape(32, 1, cols, 1)
    first = ((zl * 4 + x) * 2 + core) * share
    mine = lax.dynamic_slice_in_dim(left.reshape(32, 2, cols, rows), first, share, 3)
    mine = (mine.astype(jnp.float32) * scale).astype(jnp.bfloat16).reshape(-1, share)
    dirty_maps = lax.dot_general(mine, seen.reshape(-1, data.shape[2]), over, preferred_element_type=jnp.float32)
    right = (right.astype(jnp.float32) * scale).astype(jnp.bfloat16).reshape(-1, half)
    fisher = lax.dot_general(left.reshape(-1, rows), right, over, preferred_element_type=jnp.float32)
    return fisher, dirty_maps


def solution(mesh):
    fine = Mesh(mesh.devices.reshape(4, 4, 4, 4, 2), AXES)
    return jax.shard_map(
        step,
        mesh=fine,
        in_specs=(P(None, ("y", "zh"), ("zl", "x", "c")), P(None, ("zl", "x", "c"), None), P(), P()),
        out_specs=(P(("y", "zh"), ("zl", "x", "c")), P(AXES, None)),
        check_vma=False,
    )
```

time: 188 us -> 147 us (0.78)
  the two profiles are of different devices: /device:TPU:34 before, /device:TPU:96 now
where the time goes in v2:
time: 147 us; the launch traced here: 146 us
  blocking collectives  67.4 us (46%)
  starting transfers between devices  30.1 us (20%)
  waiting for transfers between devices  19.7 us (13%)
  local copies, waits for them, and re-layouts  18.6 us (13%)
  matrix products  6.17 us (4%)
  other arithmetic  3.03 us (2%)
    all_gather x2, blocking collectives, gather(): return lax.all_gather(block, axis, axis=0)  67.4 us
    all_to_all x1, waiting for transfers between devices, step(): right = lax.all_to_all(spread, ('y', 'x', 'c'), 0, 0)  19.6 us
    ppermute x3, starting transfers between devices, send(): return lax.ppermute(block, axis, [(i, (i + step) % 4) for i in range(4)])  10.8 us
    ppermute x4, starting transfers between devices, step(): twin = lax.ppermute(piece, 'c', [(0, 1), (1, 0)])  8.42 us
    all_to_all x1, starting transfers between devices, step(): right = lax.all_to_all(spread, ('y', 'x', 'c'), 0, 0)  7.34 us
    dynamic_update_slice x8, local copies, waits for them, and re-layouts, step(): lax.dynamic_update_slice(left, block[..., :rows], (0, place, which, 0, 0,...  6.21 us
    dynamic_update_slice x8, local copies, waits for them, and re-layouts, step(): lax.dynamic_update_slice(seen, block[..., rows:], (0, place, which, 0, 0,...  4.77 us
    dot_general x1, matrix products, step(): lax.dot_general(left.reshape(-1, rows), right, over, preferred_element_ty...  4.45 us
  transfers between devices with their start and end apart: 9, of which 1 were waited for; matrix products, arithmetic and copies ran while one was open for 13% of the time, Pallas kernels for 0%

profile of v2, /device:TPU:96, one launch (start us, length us, event | category | flops | bytes accessed | tf_op | source)
XLA Modules:
  0.0 146.0 jit_solution(4807498870531474338)
XLA Ops:
  0.6 0.0 copy-start
  0.6 3.6 %collective-permute-start = (bf16[2,64,768]{2,1,0:T(8,128)(2,1)}, bf16[2,64,768]{2,1,0:T(8,128)(2,1)S(1)}, u32[]{:S(2)}, u32[]{:S(2)}) collective-permute-start(bf16[2,64,768]{2,1,0:T(8,128)(2,1)} %bitcast.103), channel_id=1, source_target_pairs={{0,0},{8,128},{16,256},{24,384},{128,8},{136,136},{144,264},{152,3... | collective-permute-start | bytes 589832 | tf_op jit(solution)/shard_map/ppermute | solution.py:34
  4.2 1.0 pad_maximum_fusion.1
  5.2 28.4 %all-gather = bf16[8,64,896]{2,1,0:T(8,128)(2,1)} all-gather(bf16[2,64,896]{2,1,0:T(8,128)(2,1)S(1)} %pad_maximum_fusion.1), channel_id=2, replica_groups=mesh['y'=4,'zh'=4,'zl'=4,'x'=4,'c'=2] {'zl'}, dimensions={0}, use_global_device_ids=true | all-gather | bytes 1146880 | tf_op jit(solution)/shard_map/all_gather | solution.py:14
  33.6 3.4 %collective-permute-start.2 = (bf16[4,2,64,896]{3,2,1,0:T(8,128)(2,1)}, bf16[4,2,64,896]{3,2,1,0:T(8,128)(2,1)}, u32[]{:S(2)}, u32[]{:S(2)}) collective-permute-start(bf16[4,2,64,896]{3,2,1,0:T(8,128)(2,1)} %bitcast.1), channel_id=1, source_target_pairs={{0,2},{2,4},{4,6},{6,0},{1,3},{3,5},{5,7},{7,1},{8,10},{10,12},{12... | collective-permute-start | bytes 2752520 | tf_op jit(solution)/shard_map/ppermute | solution.py:10
  37.0 3.7 %collective-permute-start.4 = (bf16[4,2,64,896]{3,2,1,0:T(8,128)(2,1)}, bf16[4,2,64,896]{3,2,1,0:T(8,128)(2,1)}, u32[]{:S(2)}, u32[]{:S(2)}) collective-permute-start(bf16[4,2,64,896]{3,2,1,0:T(8,128)(2,1)} %bitcast.1), channel_id=1, source_target_pairs={{0,6},{2,0},{4,2},{6,4},{1,7},{3,1},{5,3},{7,5},{8,14},{10,8},{12,... | collective-permute-start | bytes 2752520 | tf_op jit(solution)/shard_map/ppermute | solution.py:10
  40.7 3.7 %collective-permute-start.6 = (bf16[4,2,64,896]{3,2,1,0:T(8,128)(2,1)}, bf16[4,2,64,896]{3,2,1,0:T(8,128)(2,1)}, u32[]{:S(2)}, u32[]{:S(2)}) collective-permute-start(bf16[4,2,64,896]{3,2,1,0:T(8,128)(2,1)} %bitcast.1), channel_id=1, source_target_pairs={{0,4},{2,6},{4,0},{6,2},{1,5},{3,7},{5,1},{7,3},{8,12},{10,14},{12... | collective-permute-start | bytes 2752520 | tf_op jit(solution)/shard_map/ppermute | solution.py:10
  44.4 0.7 broadcast_shift-right-arithmetic_fusion
  45.1 0.0 collective-permute-done
  45.1 38.9 %all-gather.1 = bf16[8,64,768]{2,1,0:T(8,128)(2,1)S(1)} all-gather(bf16[2,64,768]{2,1,0:T(8,128)(2,1)S(1)} %collective-permute-done), channel_id=3, replica_groups=mesh['y'=4,'zh'=4,'zl'=4,'x'=4,'c'=2] {'zh'}, dimensions={0}, use_global_device_ids=true | all-gather | bytes 983040 | tf_op jit(solution)/shard_map/all_gather | solution.py:14
  84.1 1.9 %collective-permute-start.1 = (bf16[4,2,64,896]{3,2,1,0:T(8,128)(2,1)}, bf16[4,2,64,896]{3,2,1,0:T(8,128)(2,1)}, u32[]{:S(2)}, u32[]{:S(2)}) collective-permute-start(bf16[4,2,64,896]{3,2,1,0:T(8,128)(2,1)} %bitcast.1), channel_id=1, source_target_pairs={{0,1},{1,0},{2,3},{3,2},{4,5},{5,4},{6,7},{7,6},{8,9},{9,8},{10,11... | collective-permute-start | bytes 2752520 | tf_op jit(solution)/shard_map/ppermute | solution.py:49
  86.0 0.7 fusion.1
  86.8 0.1 mul.27
  86.8 0.1 slice_bitcast_fusion.8
  87.0 0.1 pad_maximum_fusion
  87.1 0.1 copy.29
  87.2 2.2 %broadcast_in_dim.48 = bf16[4,4,2,2,64,384]{5,4,3,2,1,0:T(8,128)(2,1)} broadcast(bf16[4,2,2,64,384]{4,3,2,1,0:T(8,128)(2,1)S(1)} %copy.29), dimensions={1,2,3,4,5} | broadcast | bytes 3932160 | tf_op jit(solution)/shard_map/broadcast_in_dim | solution.py:42
  89.4 7.3 %all-to-all-start = ((bf16[32,2,64,384]{3,2,1,0:T(8,128)(2,1)}), bf16[32,2,64,384]{3,2,1,0:T(8,128)(2,1)S(1)}, u32[]{:S(2)}, u32[]{:S(2)}) async-start(bf16[32,2,64,384]{3,2,1,0:T(8,128)(2,1)} %bitcast.90), calls=%async_computation | async-start | bytes 6291456 | tf_op jit(solution)/shard_map/all_to_all | solution.py:43
  96.7 0.2 broadcast_in_dim.50
  97.0 0.9 fusion.16
  97.9 0.8 broadcast_in_dim.39
  98.7 1.2 fusion.8
  99.9 0.0 collective-permute-done.2
  99.9 2.2 %collective-permute-start.3 = (bf16[4,2,64,896]{3,2,1,0:T(8,128)(2,1)}, bf16[4,2,64,896]{3,2,1,0:T(8,128)(2,1)S(1)}, u32[]{:S(2)}, u32[]{:S(2)}) collective-permute-start(bf16[4,2,64,896]{3,2,1,0:T(8,128)(2,1)} %collective-permute-done.2), channel_id=1, source_target_pairs={{0,1},{1,0},{2,3},{3,2},{4,5},{5,4},{6,7},{7,6},{8,9},{9,8},{10,11... | collective-permute-start | bytes 2752520 | tf_op jit(solution)/shard_map/ppermute | solution.py:49
  102.1 0.0 collective-permute-done.4
  102.1 2.1 %collective-permute-start.5 = (bf16[4,2,64,896]{3,2,1,0:T(8,128)(2,1)}, bf16[4,2,64,896]{3,2,1,0:T(8,128)(2,1)S(1)}, u32[]{:S(2)}, u32[]{:S(2)}) collective-permute-start(bf16[4,2,64,896]{3,2,1,0:T(8,128)(2,1)} %collective-permute-done.4), channel_id=1, source_target_pairs={{0,1},{1,0},{2,3},{3,2},{4,5},{5,4},{6,7},{7,6},{8,9},{9,8},{10,11... | collective-permute-start | bytes 2752520 | tf_op jit(solution)/shard_map/ppermute | solution.py:49
  104.2 0.0 collective-permute-done.6
  104.2 2.2 %collective-permute-start.7 = (bf16[4,2,64,896]{3,2,1,0:T(8,128)(2,1)}, bf16[4,2,64,896]{3,2,1,0:T(8,128)(2,1)S(1)}, u32[]{:S(2)}, u32[]{:S(2)}) collective-permute-start(bf16[4,2,64,896]{3,2,1,0:T(8,128)(2,1)} %collective-permute-done.6), channel_id=1, source_target_pairs={{0,1},{1,0},{2,3},{3,2},{4,5},{5,4},{6,7},{7,6},{8,9},{9,8},{10,11... | collective-permute-start | bytes 2752520 | tf_op jit(solution)/shard_map/ppermute | solution.py:49
  106.4 0.0 collective-permute-done.1
  106.5 1.2 fusion.7
  107.7 1.2 fusion.6
  108.9 0.9 fusion.15
  109.8 0.9 fusion.14
  110.8 0.9 fusion.12
  111.7 0.0 collective-permute-done.5
  111.8 0.9 fusion.10
  112.8 0.1 fusion.5
  112.8 1.2 fusion.4
  114.1 0.1 fusion.3
  114.1 1.2 fusion.2
  115.3 0.1 slice_dynamic-update-slice_fusion
  115.4 0.6 multiply_convert_fusion.1
  116.1 2.0 %copy-done.1 = bf16[4,4,2,2,64,768]{5,4,3,2,1,0:T(8,128)(2,1)} copy-done((bf16[4,4,2,2,64,768]{5,4,3,2,1,0:T(8,128)(2,1)}, bf16[4,4,2,2,64,768]{5,4,3,2,1,0:T(8,128)(2,1)S(1)}, u32[]{:S(2)}) %copy-start.1) | copy-done | bytes 6291480
  118.1 1.0 fusion.19
  119.1 19.6 %all-to-all-done = bf16[32,2,64,384]{3,2,1,0:T(8,128)(2,1)S(1)} async-done(((bf16[32,2,64,384]{3,2,1,0:T(8,128)(2,1)}), bf16[32,2,64,384]{3,2,1,0:T(8,128)(2,1)S(1)}, u32[]{:S(2)}, u32[]{:S(2)}) %all-to-all-start) | async-done | bytes 3145760 | tf_op jit(solution)/shard_map/all_to_all | solution.py:43
  138.7 0.6 multiply_convert_fusion
  139.3 2.2 %copy-done.2 = bf16[4,4,2,2,64,768]{5,4,3,2,1,0:T(8,128)(2,1)S(1)} copy-done((bf16[4,4,2,2,64,768]{5,4,3,2,1,0:T(8,128)(2,1)S(1)}, bf16[4,4,2,2,64,768]{5,4,3,2,1,0:T(8,128)(2,1)}, u32[]{:S(2)}) %copy-start.2) | copy-done | bytes 6291480
  141.5 4.4 %fusion.18 = f32[768,384]{1,0:T(8,128)} fusion(bf16[4096,768]{1,0:T(8,128)(2,1)S(1)} %bitcast.92, bf16[4096,384]{1,0:T(8,128)(2,1)S(1)} %bitcast.95), kind=kOutput, calls=%fused_computation.45 | convolution fusion | flops 2415919104 | bytes 10616832 | tf_op jit(solution)/shard_map/dot_general | solution.py:62
  (8 shorter events, 0.1 us)
Async XLA Ops:
  0.6 85.4 %copy-start = (f32[8192]{0:T(1024)S(1)}, f32[8192]{0:T(1024)}, u32[]{:S(2)}) copy-start(f32[8192]{0:T(1024)} %param.7) | copy-start | bytes 98308
  0.6 44.5 %collective-permute-start = (bf16[2,64,768]{2,1,0:T(8,128)(2,1)}, bf16[2,64,768]{2,1,0:T(8,128)(2,1)S(1)}, u32[]{:S(2)}, u32[]{:S(2)}) collective-permute-start(bf16[2,64,768]{2,1,0:T(8,128)(2,1)} %bitcast.103), channel_id=1, source_target_pairs={{0,0},{8,128},{16,256},{24,384},{128,8},{136,136},{144,264},{152,3... | collective-permute-start | bytes 589832 | tf_op jit(solution)/shard_map/ppermute | solution.py:34
  33.6 66.2 %collective-permute-start.2 = (bf16[4,2,64,896]{3,2,1,0:T(8,128)(2,1)}, bf16[4,2,64,896]{3,2,1,0:T(8,128)(2,1)}, u32[]{:S(2)}, u32[]{:S(2)}) collective-permute-start(bf16[4,2,64,896]{3,2,1,0:T(8,128)(2,1)} %bitcast.1), channel_id=1, source_target_pairs={{0,2},{2,4},{4,6},{6,0},{1,3},{3,5},{5,7},{7,1},{8,10},{10,12},{12... | collective-permute-start | bytes 2752520 | tf_op jit(solution)/shard_map/ppermute | solution.py:10
  37.0 65.0 %collective-permute-start.4 = (bf16[4,2,64,896]{3,2,1,0:T(8,128)(2,1)}, bf16[4,2,64,896]{3,2,1,0:T(8,128)(2,1)}, u32[]{:S(2)}, u32[]{:S(2)}) collective-permute-start(bf16[4,2,64,896]{3,2,1,0:T(8,128)(2,1)} %bitcast.1), channel_id=1, source_target_pairs={{0,6},{2,0},{4,2},{6,4},{1,7},{3,1},{5,3},{7,5},{8,14},{10,8},{12,... | collective-permute-start | bytes 2752520 | tf_op jit(solution)/shard_map/ppermute | solution.py:10
  40.7 63.5 %collective-permute-start.6 = (bf16[4,2,64,896]{3,2,1,0:T(8,128)(2,1)}, bf16[4,2,64,896]{3,2,1,0:T(8,128)(2,1)}, u32[]{:S(2)}, u32[]{:S(2)}) collective-permute-start(bf16[4,2,64,896]{3,2,1,0:T(8,128)(2,1)} %bitcast.1), channel_id=1, source_target_pairs={{0,4},{2,6},{4,0},{6,2},{1,5},{3,7},{5,1},{7,3},{8,12},{10,14},{12... | collective-permute-start | bytes 2752520 | tf_op jit(solution)/shard_map/ppermute | solution.py:10
  84.1 22.4 %collective-permute-start.1 = (bf16[4,2,64,896]{3,2,1,0:T(8,128)(2,1)}, bf16[4,2,64,896]{3,2,1,0:T(8,128)(2,1)}, u32[]{:S(2)}, u32[]{:S(2)}) collective-permute-start(bf16[4,2,64,896]{3,2,1,0:T(8,128)(2,1)} %bitcast.1), channel_id=1, source_target_pairs={{0,1},{1,0},{2,3},{3,2},{4,5},{5,4},{6,7},{7,6},{8,9},{9,8},{10,11... | collective-permute-start | bytes 2752520 | tf_op jit(solution)/shard_map/ppermute | solution.py:49
  89.4 49.4 %all-to-all-start = ((bf16[32,2,64,384]{3,2,1,0:T(8,128)(2,1)}), bf16[32,2,64,384]{3,2,1,0:T(8,128)(2,1)S(1)}, u32[]{:S(2)}, u32[]{:S(2)}) async-start(bf16[32,2,64,384]{3,2,1,0:T(8,128)(2,1)} %bitcast.90), calls=%async_computation | async-start | bytes 6291456 | tf_op jit(solution)/shard_map/all_to_all | solution.py:43
  99.9 10.8 %collective-permute-start.3 = (bf16[4,2,64,896]{3,2,1,0:T(8,128)(2,1)}, bf16[4,2,64,896]{3,2,1,0:T(8,128)(2,1)S(1)}, u32[]{:S(2)}, u32[]{:S(2)}) collective-permute-start(bf16[4,2,64,896]{3,2,1,0:T(8,128)(2,1)} %collective-permute-done.2), channel_id=1, source_target_pairs={{0,1},{1,0},{2,3},{3,2},{4,5},{5,4},{6,7},{7,6},{8,9},{9,8},{10,11... | collective-permute-start | bytes 2752520 | tf_op jit(solution)/shard_map/ppermute | solution.py:49
  102.1 9.6 %collective-permute-start.5 = (bf16[4,2,64,896]{3,2,1,0:T(8,128)(2,1)}, bf16[4,2,64,896]{3,2,1,0:T(8,128)(2,1)S(1)}, u32[]{:S(2)}, u32[]{:S(2)}) collective-permute-start(bf16[4,2,64,896]{3,2,1,0:T(8,128)(2,1)} %collective-permute-done.4), channel_id=1, source_target_pairs={{0,1},{1,0},{2,3},{3,2},{4,5},{5,4},{6,7},{7,6},{8,9},{9,8},{10,11... | collective-permute-start | bytes 2752520 | tf_op jit(solution)/shard_map/ppermute | solution.py:49
  104.2 8.5 %collective-permute-start.7 = (bf16[4,2,64,896]{3,2,1,0:T(8,128)(2,1)}, bf16[4,2,64,896]{3,2,1,0:T(8,128)(2,1)S(1)}, u32[]{:S(2)}, u32[]{:S(2)}) collective-permute-start(bf16[4,2,64,896]{3,2,1,0:T(8,128)(2,1)} %collective-permute-done.6), channel_id=1, source_target_pairs={{0,1},{1,0},{2,3},{3,2},{4,5},{5,4},{6,7},{7,6},{8,9},{9,8},{10,11... | collective-permute-start | bytes 2752520 | tf_op jit(solution)/shard_map/ppermute | solution.py:49
  115.4 2.7 %copy-start.1 = (bf16[4,4,2,2,64,768]{5,4,3,2,1,0:T(8,128)(2,1)}, bf16[4,4,2,2,64,768]{5,4,3,2,1,0:T(8,128)(2,1)S(1)}, u32[]{:S(2)}) copy-start(bf16[4,4,2,2,64,768]{5,4,3,2,1,0:T(8,128)(2,1)S(1)} %slice_dynamic-update-slice_fusion) | copy-start | bytes 18874372
  138.7 2.8 %copy-start.2 = (bf16[4,4,2,2,64,768]{5,4,3,2,1,0:T(8,128)(2,1)S(1)}, bf16[4,4,2,2,64,768]{5,4,3,2,1,0:T(8,128)(2,1)}, u32[]{:S(2)}) copy-start(bf16[4,4,2,2,64,768]{5,4,3,2,1,0:T(8,128)(2,1)} %copy-done.1) | copy-start | bytes 18874372

commit v3 on v2

--- a/solution.py
+++ b/solution.py
@@ -31,15 +31,16 @@
     rows, cols = phase.shape[1], phase.shape[2]
     half = rows // 2
     local = jnp.transpose(phase, (0, 2, 1))
-    own = lax.ppermute(local, ("y", "zl"), [(4 * i + j, 4 * j + i) for i in range(4) for j in range(4)])
     line = gather(jnp.concatenate([local, data], axis=2), "zl")
+    own = lax.all_to_all(line, "y", 0, 0)
+    own = lax.dynamic_index_in_dim(own, zl, 0, keepdims=False)[..., :rows]
+    own = jnp.transpose(own.reshape(2, cols, 2, half), (2, 0, 1, 3))
     xprev = send(line, "x", 1)
     xsucc = send(line, "x", -1)
     xfar = send(line, "x", 2)
     across = gather(own, "zh")
     line, across = lax.optimization_barrier((line, across))
-    spread = jnp.stack([across[..., :half], across[..., half:]], axis=1)
-    spread = jnp.broadcast_to(spread, (4,) + spread.shape).reshape((32,) + spread.shape[2:])
+    spread = jnp.broadcast_to(across, (4,) + across.shape).reshape((32,) + across.shape[2:])
     right = lax.all_to_all(spread, ("y", "x", "c"), 0, 0)
     weight = table_rows(noise_weight, column_ids).reshape(4, 4, 2, cols)
     left = jnp.zeros((4, 4, 2) + local.shape, jnp.bfloat16)

time: 147 us -> 140 us (0.952)
  the two profiles are of different devices: /device:TPU:96 before, /device:TPU:1 now
where the time goes in v3:
time: 140 us; the launch traced here: 139 us
  blocking collectives  61.8 us (44%)
  starting transfers between devices  30.8 us (22%)
  local copies, waits for them, and re-layouts  18.6 us (13%)
  waiting for transfers between devices  17.5 us (12%)
  matrix products  6.16 us (4%)
  other arithmetic  2.94 us (2%)
    all_gather x2, blocking collectives, gather(): return lax.all_gather(block, axis, axis=0)  61.8 us
    all_to_all x1, waiting for transfers between devices, step(): right = lax.all_to_all(spread, ('y', 'x', 'c'), 0, 0)  17.5 us
    ppermute x4, starting transfers between devices, step(): twin = lax.ppermute(piece, 'c', [(0, 1), (1, 0)])  12 us
    ppermute x3, starting transfers between devices, send(): return lax.ppermute(block, axis, [(i, (i + step) % 4) for i in range(4)])  9.64 us
    dynamic_update_slice x8, local copies, waits for them, and re-layouts, step(): lax.dynamic_update_slice(left, block[..., :rows], (0, place, which, 0, 0,...  6.21 us
    all_to_all x1, starting transfers between devices, step(): right = lax.all_to_all(spread, ('y', 'x', 'c'), 0, 0)  5.67 us
    dynamic_update_slice x8, local copies, waits for them, and re-layouts, step(): lax.dynamic_update_slice(seen, block[..., rows:], (0, place, which, 0, 0,...  4.77 us
    dot_general x1, matrix products, step(): lax.dot_general(left.reshape(-1, rows), right, over, preferred_element_ty...  4.45 us
  transfers between devices with their start and end apart: 9, of which 1 were waited for; matrix products, arithmetic and copies ran while one was open for 13% of the time, Pallas kernels for 0%

profile of v3, /device:TPU:1, one launch (start us, length us, event | category | flops | bytes accessed | tf_op | source)
XLA Modules:
  0.0 138.8 jit_solution(6570463522095841956)
XLA Ops:
  0.6 0.0 copy-start
  0.6 1.0 pad_maximum_fusion
  1.6 21.5 %all-gather = bf16[8,64,896]{2,1,0:T(8,128)(2,1)} all-gather(bf16[2,64,896]{2,1,0:T(8,128)(2,1)S(1)} %pad_maximum_fusion), channel_id=2, replica_groups=mesh['y'=4,'zh'=4,'zl'=4,'x'=4,'c'=2] {'zl'}, dimensions={0}, use_global_device_ids=true | all-gather | bytes 1146880 | tf_op jit(solution)/shard_map/all_gather | solution.py:14
  23.1 3.5 %all-to-all-start = ((bf16[4,2,64,896]{3,2,1,0:T(8,128)(2,1)}), bf16[4,2,64,896]{3,2,1,0:T(8,128)(2,1)S(1)}, u32[]{:S(2)}, u32[]{:S(2)}) async-start(bf16[4,2,64,896]{3,2,1,0:T(8,128)(2,1)} %bitcast.1), calls=%async_computation | async-start | bytes 1835008 | tf_op jit(solution)/shard_map/all_to_all | solution.py:35
  26.6 2.8 %collective-permute-start.1 = (bf16[4,2,64,896]{3,2,1,0:T(8,128)(2,1)}, bf16[4,2,64,896]{3,2,1,0:T(8,128)(2,1)}, u32[]{:S(2)}, u32[]{:S(2)}) collective-permute-start(bf16[4,2,64,896]{3,2,1,0:T(8,128)(2,1)} %bitcast.1), channel_id=1, source_target_pairs={{0,2},{2,4},{4,6},{6,0},{1,3},{3,5},{5,7},{7,1},{8,10},{10,12},{12... | collective-permute-start | bytes 2752520 | tf_op jit(solution)/shard_map/ppermute | solution.py:10
  29.4 3.7 %collective-permute-start.3 = (bf16[4,2,64,896]{3,2,1,0:T(8,128)(2,1)}, bf16[4,2,64,896]{3,2,1,0:T(8,128)(2,1)}, u32[]{:S(2)}, u32[]{:S(2)}) collective-permute-start(bf16[4,2,64,896]{3,2,1,0:T(8,128)(2,1)} %bitcast.1), channel_id=1, source_target_pairs={{0,6},{2,0},{4,2},{6,4},{1,7},{3,1},{5,3},{7,5},{8,14},{10,8},{12,... | collective-permute-start | bytes 2752520 | tf_op jit(solution)/shard_map/ppermute | solution.py:10
  33.1 3.1 %collective-permute-start.5 = (bf16[4,2,64,896]{3,2,1,0:T(8,128)(2,1)}, bf16[4,2,64,896]{3,2,1,0:T(8,128)(2,1)}, u32[]{:S(2)}, u32[]{:S(2)}) collective-permute-start(bf16[4,2,64,896]{3,2,1,0:T(8,128)(2,1)} %bitcast.1), channel_id=1, source_target_pairs={{0,4},{2,6},{4,0},{6,2},{1,5},{3,7},{5,1},{7,3},{8,12},{10,14},{12... | collective-permute-start | bytes 2752520 | tf_op jit(solution)/shard_map/ppermute | solution.py:10
  36.3 0.0 all-to-all-done
  36.3 0.1 reshape.31
  36.4 40.4 %all-gather.1 = bf16[8,2,64,384]{3,2,1,0:T(8,128)(2,1)S(1)} all-gather(bf16[2,2,64,384]{3,2,1,0:T(8,128)(2,1)S(1)} %copy.35), channel_id=3, replica_groups=mesh['y'=4,'zh'=4,'zl'=4,'x'=4,'c'=2] {'zh'}, dimensions={0}, use_global_device_ids=true | all-gather | bytes 983040 | tf_op jit(solution)/shard_map/all_gather | solution.py:14
  76.8 5.5 %collective-permute-start = (bf16[4,2,64,896]{3,2,1,0:T(8,128)(2,1)}, bf16[4,2,64,896]{3,2,1,0:T(8,128)(2,1)}, u32[]{:S(2)}, u32[]{:S(2)}) collective-permute-start(bf16[4,2,64,896]{3,2,1,0:T(8,128)(2,1)} %bitcast.1), channel_id=1, source_target_pairs={{0,1},{1,0},{2,3},{3,2},{4,5},{5,4},{6,7},{7,6},{8,9},{9,8},{10,11... | collective-permute-start | bytes 2752520 | tf_op jit(solution)/shard_map/ppermute | solution.py:50
  82.4 0.7 broadcast_shift-right-arithmetic_fusion
  83.1 0.7 fusion.1
  83.8 0.1 mul.27
  83.9 2.2 %broadcast_in_dim.48 = bf16[4,4,2,2,64,384]{5,4,3,2,1,0:T(8,128)(2,1)} broadcast(bf16[4,2,2,64,384]{4,3,2,1,0:T(8,128)(2,1)S(1)} %bitcast.95), dimensions={1,2,3,4,5} | broadcast | bytes 3932160 | tf_op jit(solution)/shard_map/broadcast_in_dim | solution.py:43
  86.1 5.7 %all-to-all-start.1 = ((bf16[32,2,64,384]{3,2,1,0:T(8,128)(2,1)}), bf16[32,2,64,384]{3,2,1,0:T(8,128)(2,1)S(1)}, u32[]{:S(2)}, u32[]{:S(2)}) async-start(bf16[32,2,64,384]{3,2,1,0:T(8,128)(2,1)} %bitcast.89), calls=%async_computation.1 | async-start | bytes 6291456 | tf_op jit(solution)/shard_map/all_to_all | solution.py:44
  91.8 0.2 broadcast_in_dim.50
  92.1 0.9 fusion.16
  93.0 0.8 broadcast_in_dim.39
  93.7 1.2 fusion.8
  95.0 0.0 collective-permute-done.1
  95.0 2.1 %collective-permute-start.2 = (bf16[4,2,64,896]{3,2,1,0:T(8,128)(2,1)}, bf16[4,2,64,896]{3,2,1,0:T(8,128)(2,1)S(1)}, u32[]{:S(2)}, u32[]{:S(2)}) collective-permute-start(bf16[4,2,64,896]{3,2,1,0:T(8,128)(2,1)} %collective-permute-done.1), channel_id=1, source_target_pairs={{0,1},{1,0},{2,3},{3,2},{4,5},{5,4},{6,7},{7,6},{8,9},{9,8},{10,11... | collective-permute-start | bytes 2752520 | tf_op jit(solution)/shard_map/ppermute | solution.py:50
  97.1 0.0 collective-permute-done.3
  97.1 2.2 %collective-permute-start.4 = (bf16[4,2,64,896]{3,2,1,0:T(8,128)(2,1)}, bf16[4,2,64,896]{3,2,1,0:T(8,128)(2,1)S(1)}, u32[]{:S(2)}, u32[]{:S(2)}) collective-permute-start(bf16[4,2,64,896]{3,2,1,0:T(8,128)(2,1)} %collective-permute-done.3), channel_id=1, source_target_pairs={{0,1},{1,0},{2,3},{3,2},{4,5},{5,4},{6,7},{7,6},{8,9},{9,8},{10,11... | collective-permute-start | bytes 2752520 | tf_op jit(solution)/shard_map/ppermute | solution.py:50
  99.3 0.0 collective-permute-done.5
  99.3 2.1 %collective-permute-start.6 = (bf16[4,2,64,896]{3,2,1,0:T(8,128)(2,1)}, bf16[4,2,64,896]{3,2,1,0:T(8,128)(2,1)S(1)}, u32[]{:S(2)}, u32[]{:S(2)}) collective-permute-start(bf16[4,2,64,896]{3,2,1,0:T(8,128)(2,1)} %collective-permute-done.5), channel_id=1, source_target_pairs={{0,1},{1,0},{2,3},{3,2},{4,5},{5,4},{6,7},{7,6},{8,9},{9,8},{10,11... | collective-permute-start | bytes 2752520 | tf_op jit(solution)/shard_map/ppermute | solution.py:50
  101.5 0.0 collective-permute-done
  101.5 1.2 fusion.7
  102.7 1.2 fusion.6
  103.9 0.9 fusion.15
  104.8 0.9 fusion.14
  105.8 0.0 collective-permute-done.2
  105.8 0.9 fusion.12
  106.8 0.0 collective-permute-done.4
  106.8 0.9 fusion.10
  107.8 0.0 collective-permute-done.6
  107.8 0.1 fusion.5
  107.9 1.2 fusion.4
  109.1 0.1 fusion.3
  109.2 1.2 fusion.2
  110.4 0.1 slice_dynamic-update-slice_fusion
  110.5 0.7 multiply_convert_fusion.1
  111.1 2.0 %copy-done.1 = bf16[4,4,2,2,64,768]{5,4,3,2,1,0:T(8,128)(2,1)} copy-done((bf16[4,4,2,2,64,768]{5,4,3,2,1,0:T(8,128)(2,1)}, bf16[4,4,2,2,64,768]{5,4,3,2,1,0:T(8,128)(2,1)S(1)}, u32[]{:S(2)}) %copy-start.1) | copy-done | bytes 6291480
  113.1 1.0 fusion.19
  114.1 17.5 %all-to-all-done.1 = bf16[32,2,64,384]{3,2,1,0:T(8,128)(2,1)S(1)} async-done(((bf16[32,2,64,384]{3,2,1,0:T(8,128)(2,1)}), bf16[32,2,64,384]{3,2,1,0:T(8,128)(2,1)S(1)}, u32[]{:S(2)}, u32[]{:S(2)}) %all-to-all-start.1) | async-done | bytes 3145760 | tf_op jit(solution)/shard_map/all_to_all | solution.py:44
  131.6 0.6 multiply_convert_fusion
  132.2 2.2 %copy-done.2 = bf16[4,4,2,2,64,768]{5,4,3,2,1,0:T(8,128)(2,1)S(1)} copy-done((bf16[4,4,2,2,64,768]{5,4,3,2,1,0:T(8,128)(2,1)S(1)}, bf16[4,4,2,2,64,768]{5,4,3,2,1,0:T(8,128)(2,1)}, u32[]{:S(2)}) %copy-start.2) | copy-done | bytes 6291480
  134.4 4.4 %fusion.18 = f32[768,384]{1,0:T(8,128)} fusion(bf16[4096,768]{1,0:T(8,128)(2,1)S(1)} %bitcast.91, bf16[4096,384]{1,0:T(8,128)(2,1)S(1)} %bitcast.94), kind=kOutput, calls=%fused_computation.43 | convolution fusion | flops 2415919104 | bytes 10616832 | tf_op jit(solution)/shard_map/dot_general | solution.py:63
  (9 shorter events, 0.2 us)
Async XLA Ops:
  0.6 82.5 %copy-start = (f32[8192]{0:T(1024)S(1)}, f32[8192]{0:T(1024)}, u32[]{:S(2)}) copy-start(f32[8192]{0:T(1024)} %param.7) | copy-start | bytes 98308
  23.1 13.2 %all-to-all-start = ((bf16[4,2,64,896]{3,2,1,0:T(8,128)(2,1)}), bf16[4,2,64,896]{3,2,1,0:T(8,128)(2,1)S(1)}, u32[]{:S(2)}, u32[]{:S(2)}) async-start(bf16[4,2,64,896]{3,2,1,0:T(8,128)(2,1)} %bitcast.1), calls=%async_computation | async-start | bytes 1835008 | tf_op jit(solution)/shard_map/all_to_all | solution.py:35
  26.6 68.4 %collective-permute-start.1 = (bf16[4,2,64,896]{3,2,1,0:T(8,128)(2,1)}, bf16[4,2,64,896]{3,2,1,0:T(8,128)(2,1)}, u32[]{:S(2)}, u32[]{:S(2)}) collective-permute-start(bf16[4,2,64,896]{3,2,1,0:T(8,128)(2,1)} %bitcast.1), channel_id=1, source_target_pairs={{0,2},{2,4},{4,6},{6,0},{1,3},{3,5},{5,7},{7,1},{8,10},{10,12},{12... | collective-permute-start | bytes 2752520 | tf_op jit(solution)/shard_map/ppermute | solution.py:10
  29.4 67.7 %collective-permute-start.3 = (bf16[4,2,64,896]{3,2,1,0:T(8,128)(2,1)}, bf16[4,2,64,896]{3,2,1,0:T(8,128)(2,1)}, u32[]{:S(2)}, u32[]{:S(2)}) collective-permute-start(bf16[4,2,64,896]{3,2,1,0:T(8,128)(2,1)} %bitcast.1), channel_id=1, source_target_pairs={{0,6},{2,0},{4,2},{6,4},{1,7},{3,1},{5,3},{7,5},{8,14},{10,8},{12,... | collective-permute-start | bytes 2752520 | tf_op jit(solution)/shard_map/ppermute | solution.py:10
  33.1 66.2 %collective-permute-start.5 = (bf16[4,2,64,896]{3,2,1,0:T(8,128)(2,1)}, bf16[4,2,64,896]{3,2,1,0:T(8,128)(2,1)}, u32[]{:S(2)}, u32[]{:S(2)}) collective-permute-start(bf16[4,2,64,896]{3,2,1,0:T(8,128)(2,1)} %bitcast.1), channel_id=1, source_target_pairs={{0,4},{2,6},{4,0},{6,2},{1,5},{3,7},{5,1},{7,3},{8,12},{10,14},{12... | collective-permute-start | bytes 2752520 | tf_op jit(solution)/shard_map/ppermute | solution.py:10
  76.8 24.7 %collective-permute-start = (bf16[4,2,64,896]{3,2,1,0:T(8,128)(2,1)}, bf16[4,2,64,896]{3,2,1,0:T(8,128)(2,1)}, u32[]{:S(2)}, u32[]{:S(2)}) collective-permute-start(bf16[4,2,64,896]{3,2,1,0:T(8,128)(2,1)} %bitcast.1), channel_id=1, source_target_pairs={{0,1},{1,0},{2,3},{3,2},{4,5},{5,4},{6,7},{7,6},{8,9},{9,8},{10,11... | collective-permute-start | bytes 2752520 | tf_op jit(solution)/shard_map/ppermute | solution.py:50
  86.1 45.5 %all-to-all-start.1 = ((bf16[32,2,64,384]{3,2,1,0:T(8,128)(2,1)}), bf16[32,2,64,384]{3,2,1,0:T(8,128)(2,1)S(1)}, u32[]{:S(2)}, u32[]{:S(2)}) async-start(bf16[32,2,64,384]{3,2,1,0:T(8,128)(2,1)} %bitcast.89), calls=%async_computation.1 | async-start | bytes 6291456 | tf_op jit(solution)/shard_map/all_to_all | solution.py:44
  95.0 10.8 %collective-permute-start.2 = (bf16[4,2,64,896]{3,2,1,0:T(8,128)(2,1)}, bf16[4,2,64,896]{3,2,1,0:T(8,128)(2,1)S(1)}, u32[]{:S(2)}, u32[]{:S(2)}) collective-permute-start(bf16[4,2,64,896]{3,2,1,0:T(8,128)(2,1)} %collective-permute-done.1), channel_id=1, source_target_pairs={{0,1},{1,0},{2,3},{3,2},{4,5},{5,4},{6,7},{7,6},{8,9},{9,8},{10,11... | collective-permute-start | bytes 2752520 | tf_op jit(solution)/shard_map/ppermute | solution.py:50
  97.1 9.6 %collective-permute-start.4 = (bf16[4,2,64,896]{3,2,1,0:T(8,128)(2,1)}, bf16[4,2,64,896]{3,2,1,0:T(8,128)(2,1)S(1)}, u32[]{:S(2)}, u32[]{:S(2)}) collective-permute-start(bf16[4,2,64,896]{3,2,1,0:T(8,128)(2,1)} %collective-permute-done.3), channel_id=1, source_target_pairs={{0,1},{1,0},{2,3},{3,2},{4,5},{5,4},{6,7},{7,6},{8,9},{9,8},{10,11... | collective-permute-start | bytes 2752520 | tf_op jit(solution)/shard_map/ppermute | solution.py:50
  99.3 8.4 %collective-permute-start.6 = (bf16[4,2,64,896]{3,2,1,0:T(8,128)(2,1)}, bf16[4,2,64,896]{3,2,1,0:T(8,128)(2,1)S(1)}, u32[]{:S(2)}, u32[]{:S(2)}) collective-permute-start(bf16[4,2,64,896]{3,2,1,0:T(8,128)(2,1)} %collective-permute-done.5), channel_id=1, source_target_pairs={{0,1},{1,0},{2,3},{3,2},{4,5},{5,4},{6,7},{7,6},{8,9},{9,8},{10,11... | collective-permute-start | bytes 2752520 | tf_op jit(solution)/shard_map/ppermute | solution.py:50
  110.5 2.7 %copy-start.1 = (bf16[4,4,2,2,64,768]{5,4,3,2,1,0:T(8,128)(2,1)}, bf16[4,4,2,2,64,768]{5,4,3,2,1,0:T(8,128)(2,1)S(1)}, u32[]{:S(2)}) copy-start(bf16[4,4,2,2,64,768]{5,4,3,2,1,0:T(8,128)(2,1)S(1)} %slice_dynamic-update-slice_fusion) | copy-start | bytes 18874372
  131.6 2.8 %copy-start.2 = (bf16[4,4,2,2,64,768]{5,4,3,2,1,0:T(8,128)(2,1)S(1)}, bf16[4,4,2,2,64,768]{5,4,3,2,1,0:T(8,128)(2,1)}, u32[]{:S(2)}) copy-start(bf16[4,4,2,2,64,768]{5,4,3,2,1,0:T(8,128)(2,1)} %copy-done.1) | copy-start | bytes 18874372

commit v4 on v3

--- a/solution.py
+++ b/solution.py
@@ -40,18 +40,18 @@
     xfar = send(line, "x", 2)
     across = gather(own, "zh")
     line, across = lax.optimization_barrier((line, across))
-    spread = jnp.broadcast_to(across, (4,) + across.shape).reshape((32,) + across.shape[2:])
-    right = lax.all_to_all(spread, ("y", "x", "c"), 0, 0)
-    weight = table_rows(noise_weight, column_ids).reshape(4, 4, 2, cols)
+    spread = jnp.broadcast_to(across[:, None], (4,) + across.shape).reshape((32,) + across.shape[2:])
+    right = lax.all_to_all(spread, ("x", "y", "c"), 0, 0)
+    weight = jnp.transpose(table_rows(noise_weight, column_ids).reshape(4, 4, 2, cols), (1, 0, 2, 3))
     left = jnp.zeros((4, 4, 2) + local.shape, jnp.bfloat16)
     seen = jnp.zeros((4, 4, 2) + data.shape, jnp.bfloat16)
     for offset, piece in ((0, line), (-1, xprev), (1, xsucc), (2, xfar)):
         place = (x + offset) % 4
         twin = lax.ppermute(piece, "c", [(0, 1), (1, 0)])
         for which, block in ((core, piece), (1 - core, twin)):
-            block = block[:, None, None]
-            left = lax.dynamic_update_slice(left, block[..., :rows], (0, place, which, 0, 0, 0))
-            seen = lax.dynamic_update_slice(seen, block[..., rows:], (0, place, which, 0, 0, 0))
+            block = block[None, :, None]
+            left = lax.dynamic_update_slice(left, block[..., :rows], (place, 0, which, 0, 0, 0))
+            seen = lax.dynamic_update_slice(seen, block[..., rows:], (place, 0, which, 0, 0, 0))
     over = (((0,), (0,)), ((), ()))
     share = rows // 32
     scale = weight.reshape(32, 1, cols, 1)

time: 140 us -> 140 us (level)
  no operation moved by 1% of the time
where the time goes in v4:
time: 140 us; the launch traced here: 139 us
  blocking collectives  61.8 us (44%)
  starting transfers between devices  30.8 us (22%)
  local copies, waits for them, and re-layouts  18.6 us (13%)
  waiting for transfers between devices  17.4 us (12%)
  matrix products  6.16 us (4%)
  other arithmetic  2.94 us (2%)
    all_gather x2, blocking collectives, gather(): return lax.all_gather(block, axis, axis=0)  61.8 us
    all_to_all x1, waiting for transfers between devices, step(): right = lax.all_to_all(spread, ('x', 'y', 'c'), 0, 0)  17.4 us
    ppermute x4, starting transfers between devices, step(): twin = lax.ppermute(piece, 'c', [(0, 1), (1, 0)])  12 us
    ppermute x3, starting transfers between devices, send(): return lax.ppermute(block, axis, [(i, (i + step) % 4) for i in range(4)])  9.64 us
    dynamic_update_slice x8, local copies, waits for them, and re-layouts, step(): lax.dynamic_update_slice(left, block[..., :rows], (place, 0, which, 0, 0,...  6.21 us
    all_to_all x1, starting transfers between devices, step(): right = lax.all_to_all(spread, ('x', 'y', 'c'), 0, 0)  5.67 us
    dynamic_update_slice x8, local copies, waits for them, and re-layouts, step(): lax.dynamic_update_slice(seen, block[..., rows:], (place, 0, which, 0, 0,...  4.77 us
    dot_general x1, matrix products, step(): lax.dot_general(left.reshape(-1, rows), right, over, preferred_element_ty...  4.45 us
  transfers between devices with their start and end apart: 9, of which 1 were waited for; matrix products, arithmetic and copies ran while one was open for 13% of the time, Pallas kernels for 0%

profile of v4, /device:TPU:1, one launch (start us, length us, event | category | flops | bytes accessed | tf_op | source)
XLA Modules:
  0.0 138.8 jit_solution(1785432244049331943)
XLA Ops:
  0.6 0.0 copy-start
  0.6 1.0 pad_maximum_fusion
  1.6 21.5 %all-gather = bf16[8,64,896]{2,1,0:T(8,128)(2,1)} all-gather(bf16[2,64,896]{2,1,0:T(8,128)(2,1)S(1)} %pad_maximum_fusion), channel_id=2, replica_groups=mesh['y'=4,'zh'=4,'zl'=4,'x'=4,'c'=2] {'zl'}, dimensions={0}, use_global_device_ids=true | all-gather | bytes 1146880 | tf_op jit(solution)/shard_map/all_gather | solution.py:14
  23.1 3.5 %all-to-all-start = ((bf16[4,2,64,896]{3,2,1,0:T(8,128)(2,1)}), bf16[4,2,64,896]{3,2,1,0:T(8,128)(2,1)S(1)}, u32[]{:S(2)}, u32[]{:S(2)}) async-start(bf16[4,2,64,896]{3,2,1,0:T(8,128)(2,1)} %bitcast.1), calls=%async_computation | async-start | bytes 1835008 | tf_op jit(solution)/shard_map/all_to_all | solution.py:35
  26.6 2.8 %collective-permute-start.1 = (bf16[4,2,64,896]{3,2,1,0:T(8,128)(2,1)}, bf16[4,2,64,896]{3,2,1,0:T(8,128)(2,1)}, u32[]{:S(2)}, u32[]{:S(2)}) collective-permute-start(bf16[4,2,64,896]{3,2,1,0:T(8,128)(2,1)} %bitcast.1), channel_id=1, source_target_pairs={{0,2},{2,4},{4,6},{6,0},{1,3},{3,5},{5,7},{7,1},{8,10},{10,12},{12... | collective-permute-start | bytes 2752520 | tf_op jit(solution)/shard_map/ppermute | solution.py:10
  29.4 3.7 %collective-permute-start.3 = (bf16[4,2,64,896]{3,2,1,0:T(8,128)(2,1)}, bf16[4,2,64,896]{3,2,1,0:T(8,128)(2,1)}, u32[]{:S(2)}, u32[]{:S(2)}) collective-permute-start(bf16[4,2,64,896]{3,2,1,0:T(8,128)(2,1)} %bitcast.1), channel_id=1, source_target_pairs={{0,6},{2,0},{4,2},{6,4},{1,7},{3,1},{5,3},{7,5},{8,14},{10,8},{12,... | collective-permute-start | bytes 2752520 | tf_op jit(solution)/shard_map/ppermute | solution.py:10
  33.1 3.1 %collective-permute-start.5 = (bf16[4,2,64,896]{3,2,1,0:T(8,128)(2,1)}, bf16[4,2,64,896]{3,2,1,0:T(8,128)(2,1)}, u32[]{:S(2)}, u32[]{:S(2)}) collective-permute-start(bf16[4,2,64,896]{3,2,1,0:T(8,128)(2,1)} %bitcast.1), channel_id=1, source_target_pairs={{0,4},{2,6},{4,0},{6,2},{1,5},{3,7},{5,1},{7,3},{8,12},{10,14},{12... | collective-permute-start | bytes 2752520 | tf_op jit(solution)/shard_map/ppermute | solution.py:10
  36.3 0.0 all-to-all-done
  36.3 0.1 reshape.36
  36.4 40.4 %all-gather.1 = bf16[8,2,64,384]{3,2,1,0:T(8,128)(2,1)S(1)} all-gather(bf16[2,2,64,384]{3,2,1,0:T(8,128)(2,1)S(1)} %copy.36), channel_id=3, replica_groups=mesh['y'=4,'zh'=4,'zl'=4,'x'=4,'c'=2] {'zh'}, dimensions={0}, use_global_device_ids=true | all-gather | bytes 983040 | tf_op jit(solution)/shard_map/all_gather | solution.py:14
  76.8 5.5 %collective-permute-start = (bf16[4,2,64,896]{3,2,1,0:T(8,128)(2,1)}, bf16[4,2,64,896]{3,2,1,0:T(8,128)(2,1)}, u32[]{:S(2)}, u32[]{:S(2)}) collective-permute-start(bf16[4,2,64,896]{3,2,1,0:T(8,128)(2,1)} %bitcast.1), channel_id=1, source_target_pairs={{0,1},{1,0},{2,3},{3,2},{4,5},{5,4},{6,7},{7,6},{8,9},{9,8},{10,11... | collective-permute-start | bytes 2752520 | tf_op jit(solution)/shard_map/ppermute | solution.py:50
  82.4 0.7 broadcast_shift-right-arithmetic_fusion
  83.1 0.7 fusion.1
  83.8 0.1 reshape.40
  83.9 2.2 %broadcast_in_dim.51 = bf16[4,4,2,2,64,384]{5,4,3,2,1,0:T(8,128)(2,1)} broadcast(bf16[4,2,2,64,384]{4,3,2,1,0:T(8,128)(2,1)S(1)} %bitcast.97), dimensions={0,2,3,4,5} | broadcast | bytes 3932160 | tf_op jit(solution)/shard_map/broadcast_in_dim | solution.py:43
  86.2 5.7 %all-to-all-start.1 = ((bf16[32,2,64,384]{3,2,1,0:T(8,128)(2,1)}), bf16[32,2,64,384]{3,2,1,0:T(8,128)(2,1)S(1)}, u32[]{:S(2)}, u32[]{:S(2)}) async-start(bf16[32,2,64,384]{3,2,1,0:T(8,128)(2,1)} %bitcast.91), calls=%async_computation.1 | async-start | bytes 6291456 | tf_op jit(solution)/shard_map/all_to_all | solution.py:44
  91.8 0.2 broadcast_in_dim.53
  92.1 0.9 fusion.16
  93.0 0.8 broadcast_in_dim.42
  93.8 1.2 fusion.8
  95.0 0.0 collective-permute-done.1
  95.0 2.1 %collective-permute-start.2 = (bf16[4,2,64,896]{3,2,1,0:T(8,128)(2,1)}, bf16[4,2,64,896]{3,2,1,0:T(8,128)(2,1)S(1)}, u32[]{:S(2)}, u32[]{:S(2)}) collective-permute-start(bf16[4,2,64,896]{3,2,1,0:T(8,128)(2,1)} %collective-permute-done.1), channel_id=1, source_target_pairs={{0,1},{1,0},{2,3},{3,2},{4,5},{5,4},{6,7},{7,6},{8,9},{9,8},{10,11... | collective-permute-start | bytes 2752520 | tf_op jit(solution)/shard_map/ppermute | solution.py:50
  97.2 0.0 collective-permute-done.3
  97.2 2.2 %collective-permute-start.4 = (bf16[4,2,64,896]{3,2,1,0:T(8,128)(2,1)}, bf16[4,2,64,896]{3,2,1,0:T(8,128)(2,1)S(1)}, u32[]{:S(2)}, u32[]{:S(2)}) collective-permute-start(bf16[4,2,64,896]{3,2,1,0:T(8,128)(2,1)} %collective-permute-done.3), channel_id=1, source_target_pairs={{0,1},{1,0},{2,3},{3,2},{4,5},{5,4},{6,7},{7,6},{8,9},{9,8},{10,11... | collective-permute-start | bytes 2752520 | tf_op jit(solution)/shard_map/ppermute | solution.py:50
  99.4 0.0 collective-permute-done.5
  99.4 2.1 %collective-permute-start.6 = (bf16[4,2,64,896]{3,2,1,0:T(8,128)(2,1)}, bf16[4,2,64,896]{3,2,1,0:T(8,128)(2,1)S(1)}, u32[]{:S(2)}, u32[]{:S(2)}) collective-permute-start(bf16[4,2,64,896]{3,2,1,0:T(8,128)(2,1)} %collective-permute-done.5), channel_id=1, source_target_pairs={{0,1},{1,0},{2,3},{3,2},{4,5},{5,4},{6,7},{7,6},{8,9},{9,8},{10,11... | collective-permute-start | bytes 2752520 | tf_op jit(solution)/shard_map/ppermute | solution.py:50
  101.5 0.0 collective-permute-done
  101.5 1.2 fusion.7
  102.7 1.2 fusion.6
  104.0 0.9 fusion.15
  104.9 0.9 fusion.14
  105.8 0.0 collective-permute-done.2
  105.9 0.9 fusion.12
  106.8 0.0 collective-permute-done.4
  106.9 0.9 fusion.10
  107.8 0.0 collective-permute-done.6
  107.9 0.1 fusion.5
  107.9 1.2 fusion.4
  109.1 0.1 fusion.3
  109.2 1.2 fusion.2
  110.4 0.1 slice_dynamic-update-slice_fusion
  110.5 0.7 multiply_convert_fusion.1
  111.2 2.0 %copy-done.1 = bf16[4,4,2,2,64,768]{5,4,3,2,1,0:T(8,128)(2,1)} copy-done((bf16[4,4,2,2,64,768]{5,4,3,2,1,0:T(8,128)(2,1)}, bf16[4,4,2,2,64,768]{5,4,3,2,1,0:T(8,128)(2,1)S(1)}, u32[]{:S(2)}) %copy-start.1) | copy-done | bytes 6291480
  113.2 1.0 fusion.19
  114.2 17.4 %all-to-all-done.1 = bf16[32,2,64,384]{3,2,1,0:T(8,128)(2,1)S(1)} async-done(((bf16[32,2,64,384]{3,2,1,0:T(8,128)(2,1)}), bf16[32,2,64,384]{3,2,1,0:T(8,128)(2,1)S(1)}, u32[]{:S(2)}, u32[]{:S(2)}) %all-to-all-start.1) | async-done | bytes 3145760 | tf_op jit(solution)/shard_map/all_to_all | solution.py:44
  131.6 0.6 multiply_convert_fusion
  132.2 2.2 %copy-done.2 = bf16[4,4,2,2,64,768]{5,4,3,2,1,0:T(8,128)(2,1)S(1)} copy-done((bf16[4,4,2,2,64,768]{5,4,3,2,1,0:T(8,128)(2,1)S(1)}, bf16[4,4,2,2,64,768]{5,4,3,2,1,0:T(8,128)(2,1)}, u32[]{:S(2)}) %copy-start.2) | copy-done | bytes 6291480
  134.4 4.4 %fusion.18 = f32[768,384]{1,0:T(8,128)} fusion(bf16[4096,768]{1,0:T(8,128)(2,1)S(1)} %bitcast.93, bf16[4096,384]{1,0:T(8,128)(2,1)S(1)} %bitcast.96), kind=kOutput, calls=%fused_computation.43 | convolution fusion | flops 2415919104 | bytes 10616832 | tf_op jit(solution)/shard_map/dot_general | solution.py:63
  (10 shorter events, 0.2 us)
Async XLA Ops:
  0.6 82.5 %copy-start = (f32[8192]{0:T(1024)S(1)}, f32[8192]{0:T(1024)}, u32[]{:S(2)}) copy-start(f32[8192]{0:T(1024)} %param.7) | copy-start | bytes 98308
  23.1 13.2 %all-to-all-start = ((bf16[4,2,64,896]{3,2,1,0:T(8,128)(2,1)}), bf16[4,2,64,896]{3,2,1,0:T(8,128)(2,1)S(1)}, u32[]{:S(2)}, u32[]{:S(2)}) async-start(bf16[4,2,64,896]{3,2,1,0:T(8,128)(2,1)} %bitcast.1), calls=%async_computation | async-start | bytes 1835008 | tf_op jit(solution)/shard_map/all_to_all | solution.py:35
  26.6 68.4 %collective-permute-start.1 = (bf16[4,2,64,896]{3,2,1,0:T(8,128)(2,1)}, bf16[4,2,64,896]{3,2,1,0:T(8,128)(2,1)}, u32[]{:S(2)}, u32[]{:S(2)}) collective-permute-start(bf16[4,2,64,896]{3,2,1,0:T(8,128)(2,1)} %bitcast.1), channel_id=1, source_target_pairs={{0,2},{2,4},{4,6},{6,0},{1,3},{3,5},{5,7},{7,1},{8,10},{10,12},{12... | collective-permute-start | bytes 2752520 | tf_op jit(solution)/shard_map/ppermute | solution.py:10
  29.4 67.7 %collective-permute-start.3 = (bf16[4,2,64,896]{3,2,1,0:T(8,128)(2,1)}, bf16[4,2,64,896]{3,2,1,0:T(8,128)(2,1)}, u32[]{:S(2)}, u32[]{:S(2)}) collective-permute-start(bf16[4,2,64,896]{3,2,1,0:T(8,128)(2,1)} %bitcast.1), channel_id=1, source_target_pairs={{0,6},{2,0},{4,2},{6,4},{1,7},{3,1},{5,3},{7,5},{8,14},{10,8},{12,... | collective-permute-start | bytes 2752520 | tf_op jit(solution)/shard_map/ppermute | solution.py:10
  33.1 66.3 %collective-permute-start.5 = (bf16[4,2,64,896]{3,2,1,0:T(8,128)(2,1)}, bf16[4,2,64,896]{3,2,1,0:T(8,128)(2,1)}, u32[]{:S(2)}, u32[]{:S(2)}) collective-permute-start(bf16[4,2,64,896]{3,2,1,0:T(8,128)(2,1)} %bitcast.1), channel_id=1, source_target_pairs={{0,4},{2,6},{4,0},{6,2},{1,5},{3,7},{5,1},{7,3},{8,12},{10,14},{12... | collective-permute-start | bytes 2752520 | tf_op jit(solution)/shard_map/ppermute | solution.py:10
  76.8 24.7 %collective-permute-start = (bf16[4,2,64,896]{3,2,1,0:T(8,128)(2,1)}, bf16[4,2,64,896]{3,2,1,0:T(8,128)(2,1)}, u32[]{:S(2)}, u32[]{:S(2)}) collective-permute-start(bf16[4,2,64,896]{3,2,1,0:T(8,128)(2,1)} %bitcast.1), channel_id=1, source_target_pairs={{0,1},{1,0},{2,3},{3,2},{4,5},{5,4},{6,7},{7,6},{8,9},{9,8},{10,11... | collective-permute-start | bytes 2752520 | tf_op jit(solution)/shard_map/ppermute | solution.py:50
  86.2 45.4 %all-to-all-start.1 = ((bf16[32,2,64,384]{3,2,1,0:T(8,128)(2,1)}), bf16[32,2,64,384]{3,2,1,0:T(8,128)(2,1)S(1)}, u32[]{:S(2)}, u32[]{:S(2)}) async-start(bf16[32,2,64,384]{3,2,1,0:T(8,128)(2,1)} %bitcast.91), calls=%async_computation.1 | async-start | bytes 6291456 | tf_op jit(solution)/shard_map/all_to_all | solution.py:44
  95.0 10.8 %collective-permute-start.2 = (bf16[4,2,64,896]{3,2,1,0:T(8,128)(2,1)}, bf16[4,2,64,896]{3,2,1,0:T(8,128)(2,1)S(1)}, u32[]{:S(2)}, u32[]{:S(2)}) collective-permute-start(bf16[4,2,64,896]{3,2,1,0:T(8,128)(2,1)} %collective-permute-done.1), channel_id=1, source_target_pairs={{0,1},{1,0},{2,3},{3,2},{4,5},{5,4},{6,7},{7,6},{8,9},{9,8},{10,11... | collective-permute-start | bytes 2752520 | tf_op jit(solution)/shard_map/ppermute | solution.py:50
  97.2 9.6 %collective-permute-start.4 = (bf16[4,2,64,896]{3,2,1,0:T(8,128)(2,1)}, bf16[4,2,64,896]{3,2,1,0:T(8,128)(2,1)S(1)}, u32[]{:S(2)}, u32[]{:S(2)}) collective-permute-start(bf16[4,2,64,896]{3,2,1,0:T(8,128)(2,1)} %collective-permute-done.3), channel_id=1, source_target_pairs={{0,1},{1,0},{2,3},{3,2},{4,5},{5,4},{6,7},{7,6},{8,9},{9,8},{10,11... | collective-permute-start | bytes 2752520 | tf_op jit(solution)/shard_map/ppermute | solution.py:50
  99.4 8.4 %collective-permute-start.6 = (bf16[4,2,64,896]{3,2,1,0:T(8,128)(2,1)}, bf16[4,2,64,896]{3,2,1,0:T(8,128)(2,1)S(1)}, u32[]{:S(2)}, u32[]{:S(2)}) collective-permute-start(bf16[4,2,64,896]{3,2,1,0:T(8,128)(2,1)} %collective-permute-done.5), channel_id=1, source_target_pairs={{0,1},{1,0},{2,3},{3,2},{4,5},{5,4},{6,7},{7,6},{8,9},{9,8},{10,11... | collective-permute-start | bytes 2752520 | tf_op jit(solution)/shard_map/ppermute | solution.py:50
  110.5 2.7 %copy-start.1 = (bf16[4,4,2,2,64,768]{5,4,3,2,1,0:T(8,128)(2,1)}, bf16[4,4,2,2,64,768]{5,4,3,2,1,0:T(8,128)(2,1)S(1)}, u32[]{:S(2)}) copy-start(bf16[4,4,2,2,64,768]{5,4,3,2,1,0:T(8,128)(2,1)S(1)} %slice_dynamic-update-slice_fusion) | copy-start | bytes 18874372
  131.6 2.8 %copy-start.2 = (bf16[4,4,2,2,64,768]{5,4,3,2,1,0:T(8,128)(2,1)S(1)}, bf16[4,4,2,2,64,768]{5,4,3,2,1,0:T(8,128)(2,1)}, u32[]{:S(2)}) copy-start(bf16[4,4,2,2,64,768]{5,4,3,2,1,0:T(8,128)(2,1)} %copy-done.1) | copy-start | bytes 18874372
